TPU v7x, 32 devices: a whole 2x2x4 slice. The times are simulated.
32 devices in a mesh: row: 8 (over z, x), col: 4 (over y, core).
Axes of the slice: x: 2, y: 2, z: 4, core: 2. Of those that a mesh axis runs over, the one named last changes fastest.
Arguments:
- charge_drive: float32 [128, 16, 128], P(('row', 'col')), may hold values from -6 to 6
- hardness: float32 [128, 128], P(('row', 'col')), may hold values from 1 to 4
- bond_stiffness: float32 [256, 128], P('row'), may hold values from 0.5 to 4
- coulomb_tiles: float32 [4096, 128, 128], P(('row', 'col')), may hold values from -0.01 to 0.01
- tile_rows: int32 [4096], P(('row', 'col')), may hold values from 0 to 31
- tile_cols: int32 [4096], P(('row', 'col')), may hold values from 0 to 15
- tile_count: int32 [32], P(('row', 'col')), may hold values from 25 to 128, as said below
- link_bonds: int32 [1024], P(('row', 'col')), may hold values from 0 to 31, as said below
- link_cells: int32 [1024], P(('row', 'col')), may hold values from 0 to 31
- link_ends: int32 [1024, 2, 128], P(('row', 'col')), may hold values from 0 to 127, as said below
- link_carry: int32 [1024, 128], P(('row', 'col')), may hold values from 0 to 1, as said below
- link_count: int32 [32], P(('row', 'col')), may hold values from 8 to 32, as said below
Outputs:
- solution: float32 [256, 16, 128], P(('row', 'col'))
- residual: float32 [256, 16, 128], P(('row', 'col'))
Inputs may be any that keep to these rules, and one draw needn't show every extreme that they name: `tile_count`: live tile slots of each device, the busiest device has exactly 128. `link_count`: live incidence slots of each device, the busiest device has exactly 32. `link_bonds`: within each row of devices, every bond of every one of the row's bond blocks is carried by exactly one live incidence slot. `link_carry`: dead slots carry nothing. `link_ends`: the two ends of every bond are distinct atoms.
All inputs are finite; a program needn't handle non-finite values.
Results may differ from a plain program's by a relative error of at most 0.00022.
Values sent between devices are 32-bit elements; how exact they have to be, the bound alone decides.
A program may use at most 64 MiB of HBM per device.

v0:
```python
import functools

import jax
import jax.numpy as jnp
from jax import lax
from jax.experimental import pallas as pl
from jax.experimental.pallas import tpu as pltpu
from jax.sharding import PartitionSpec as P

MESH = pl.DeviceIdType.MESH
NT = (((1,), (1,)), ((), ()))
NN = (((1,), (0,)), ((), ()))


def halves(value):
    high = value.astype(jnp.bfloat16)
    low = (value - high.astype(jnp.float32)).astype(jnp.bfloat16)
    return high, low


def dot(left, right, dims=NN):
    return lax.dot_general(left, right, dims, preferred_element_type=jnp.float32)


def order_kernel(tile_rows, tile_cols, link_bonds, link_cells, tiles_live, links_live, table, ids, sem):
    width = ids.shape[1]
    ids[...] = jnp.zeros_like(ids)
    copies = []
    for i, (source, target) in enumerate((
        (tile_rows, ids.at[0:1, 0 : tile_rows.shape[1]]), (tile_cols, ids.at[1:2, 0 : tile_cols.shape[1]]),
    )):
        copy = pltpu.make_async_copy(source, target, sem.at[i])
        copy.start()
        copies.append(copy)
    ids[2:3, 0 : link_bonds.shape[1]] = link_bonds[...]
    ids[3:4, 0 : link_cells.shape[1]] = link_cells[...]
    for copy in copies:
        copy.wait()
    beyond = 1 << 20
    down = lax.broadcasted_iota(jnp.int32, (width, width), 0)
    across = lax.broadcasted_iota(jnp.int32, (width, width), 1)

    def total(value, axis):
        return jnp.sum(value, axis=axis, keepdims=True)

    def column(row):
        return total(jnp.where(down == across, row, 0), 1)

    tile_count, link_count = tiles_live[0], links_live[0]
    for place, (row, other, count) in enumerate((
        (0, 1, tile_count), (1, 0, tile_count), (3, 3, link_count), (2, 2, link_count),
    )):
        key = jnp.where(across[0:1] < count, ids[row : row + 1, :], beyond)
        mine = column(key)
        equal_before = total(jnp.where((key == mine) & (across < down), 1, 0), 1)
        rank = total(jnp.where(key < mine, 1, 0), 1) + equal_before
        here = rank == across
        upto = total(jnp.where(mine <= across, 1, 0), 0)
        fewer = total(jnp.where(mine < across, 1, 0), 0)
        at = 5 * place
        table[at : at + 1, :] = total(jnp.where(here, down, 0), 0)
        table[at + 1 : at + 2, :] = total(jnp.where(here & (equal_before > 0), 1, 0), 0)
        table[at + 2 : at + 3, :] = jnp.maximum(upto - 1, 0)
        table[at + 3 : at + 4, :] = jnp.where(upto > fewer, 1, 0)
        table[at + 4 : at + 5, :] = total(jnp.where(here, column(ids[other : other + 1, :]), 0), 0)
    table[20:22, :] = ids[2:4, :]
    table[22:24, :] = jnp.full((2, width), link_count, jnp.int32)


def kernel(
    rows, cols, sizes,
    table, drive, hardness_hbm, stiffness_hbm, tiles_hbm, ends_hbm, carry_hbm,
    out_solution, out_residual,
    hardness, stiffness, ends, carry,
    tiles, tile_parts, incidence, u0, u1, u2, products, slot_products, bond_products,
    drive_all, charge_part, charge_in, row_charge, col_charge,
    row_parts, col_parts, pot_part, pot_in, mirror_part, mirror_in, pot_all, pot_parts,
    bond_part, bond_in, dots_row, dots_col,
    small_sem, tile_sem, row_send, row_recv, col_send, col_recv,
):
    cells_dev, sets, lanes, tile_slots, link_slots, row_bonds = sizes
    group_cells, row_cells = rows * cells_dev, cols * cells_dev
    share = row_bonds // cols
    block = cells_dev * sets
    r, c = lax.axis_index("row"), lax.axis_index("col")

    small = []
    for i, (source, target) in enumerate((
        (ends_hbm, ends), (carry_hbm, carry),
        (hardness_hbm, hardness), (stiffness_hbm, stiffness), (drive, drive_all.at[r]),
    )):
        copy = pltpu.make_async_copy(source, target, small_sem.at[i])
        copy.start()
        small.append(copy)
    chunks = tile_sem.shape[0]
    per_chunk = tile_slots // chunks
    tile_copies = []
    for i in range(chunks):
        part = pl.ds(i * per_chunk, per_chunk)
        copy = pltpu.make_async_copy(tiles_hbm.at[part], tiles.at[part], tile_sem.at[i])
        copy.start()
        tile_copies.append(copy)

    barrier = pltpu.get_barrier_semaphore()
    for k in range(1, rows):
        pl.semaphore_signal(barrier, inc=1, device_id=(lax.rem(r + k, rows), c), device_id_type=MESH)
    for k in range(1, cols):
        pl.semaphore_signal(barrier, inc=1, device_id=(r, lax.rem(c + k, cols)), device_id_type=MESH)
    pl.semaphore_wait(barrier, rows + cols - 2)

    started = []

    def send_row(phase, source, target):
        copies = []
        for k in range(1, rows):
            peer = lax.rem(r + k, rows)
            copy = pltpu.make_async_remote_copy(
                src_ref=source(peer), dst_ref=target,
                send_sem=row_send.at[phase, k], recv_sem=row_recv.at[phase, k],
                device_id=(peer, c), device_id_type=MESH,
            )
            copy.start()
            copies.append(copy)
        started.extend(copies)
        return copies

    def send_col(phase, source, target):
        copies = []
        for k in range(1, cols):
            peer = lax.rem(c + k, cols)
            copy = pltpu.make_async_remote_copy(
                src_ref=source(peer), dst_ref=target,
                send_sem=col_send.at[phase, k], recv_sem=col_recv.at[phase, k],
                device_id=(r, peer), device_id_type=MESH,
            )
            copy.start()
            copies.append(copy)
        started.extend(copies)
        return copies

    def arrive(copies):
        for copy in copies:
            copy.wait_recv()

    inner = 2 if rows % 2 == 0 else 1
    outer = rows // inner
    high_row, low_row = r // inner, lax.rem(r, inner)

    def row_copy(phase, index, source, target, peer):
        copy = pltpu.make_async_remote_copy(
            src_ref=source, dst_ref=target,
            send_sem=row_send.at[phase, index], recv_sem=row_recv.at[phase, index],
            device_id=(peer, c), device_id_type=MESH,
        )
        copy.start()
        started.append(copy)
        return copy

    def gather_begin(phase, source, slot_of):
        far = [
            row_copy(phase, k * inner, source, slot_of(r), lax.rem(high_row + k, outer) * inner + low_row)
            for k in range(1, outer)
        ]
        near = [
            row_copy(phase, 1, source, slot_of(r), high_row * inner + 1 - low_row)
            for _ in range(inner - 1)
        ]
        return far, near

    def gather_end(phase, copies, slot_of):
        far, near = copies
        for k, copy in enumerate(far, 1):
            copy.wait_recv()
            if inner > 1:
                block_row = lax.rem(high_row + outer - k, outer) * inner + low_row
                near.append(row_copy(
                    phase, k * inner + 1, slot_of(block_row), slot_of(block_row),
                    high_row * inner + 1 - low_row,
                ))
        arrive(near)

    drive_copies = gather_begin(0, drive, lambda row: drive_all.at[row])
    link_count = table[22, 0]
    small[0].wait()
    small[1].wait()

    def build_incidence(s, _):
        atom = lax.broadcasted_iota(jnp.int32, (lanes, lanes), 0)
        pair = ends[s]
        live = jnp.full((1, lanes), s, jnp.int32) < link_count
        kept = jnp.where(live, carry[pl.ds(s, 1), :], 0).astype(jnp.float32)
        gain = jnp.where(atom == pair[0:1, :], kept, 0.0)
        lose = jnp.where(atom == pair[1:2, :], kept, 0.0)
        incidence[s] = (gain - lose).astype(jnp.bfloat16)
        return 0

    lax.fori_loop(0, link_slots, build_incidence, 0)
    for copy in small[2:]:
        copy.wait()

    def split_tiles(t, _):
        high, low = halves(tiles[t])
        tile_parts[t, 0:lanes, :] = high
        tile_parts[t, lanes : 2 * lanes, :] = low
        return 0

    def add_slots(place, slots, size, value, running, target):
        def body(i, carried):
            for j in range(UNROLL):
                k = i * UNROLL + j
                kept = jnp.full((sets, lanes), table[5 * place + 1, k], jnp.int32).astype(jnp.float32)
                carried = carried * kept + value(k, table[5 * place, k], table[5 * place + 4, k])
                running[k] = carried
            return carried

        lax.fori_loop(0, slots // UNROLL, body, jnp.zeros((sets, lanes), jnp.float32))

        def spread(i, _):
            for j in range(4):
                l = i * 4 + j
                some = jnp.full((sets, lanes), table[5 * place + 3, l], jnp.int32).astype(jnp.float32)
                found = running[table[5 * place + 2, l]]
                target[slot(l), :] = found * some
            return 0

        lax.fori_loop(0, size // 4, spread, 0)

    UNROLL = 32

    def to_bonds(potential_of, update):
        def fill(l, _):
            high, low = halves(potential_of(l))
            pot_parts[l, 0:sets, :] = high
            pot_parts[l, sets : 2 * sets, :] = low
            return 0

        lax.fori_loop(0, group_cells, fill, 0)

        def body(i, _):
            for j in range(UNROLL):
                s = i * UNROLL + j
                both = dot(pot_parts[table[21, s]], incidence[s])
                update(s, both[0:sets] + both[sets : 2 * sets])
            return 0

        lax.fori_loop(0, link_slots // UNROLL, body, 0)

    def to_charges(n, u):
        def value(k, s, _):
            high, low = halves(u[s])
            both = dot(jnp.concatenate([high, low], axis=0), incidence[s], NT)
            return both[0:sets] + both[sets : 2 * sets]

        add_slots(2, link_slots, group_cells, value, slot_products, charge_part.at[n])

    def slot(s):
        return pl.ds(pl.multiple_of(s * sets, sets), sets)

    def send_bonds(n, u):
        add_slots(3, link_slots, row_bonds, lambda k, s, _: u[s], bond_products, bond_part.at[n])
        size = share * sets
        copies = send_col(
            4 + n,
            lambda peer: bond_part.at[n, pl.ds(pl.multiple_of(peer * size, size), size)],
            bond_in.at[n, c],
        )
        bond_in[n, c] = bond_part[n, pl.ds(pl.multiple_of(c * size, size), size), :]
        return copies

    gather_end(0, drive_copies, lambda row: drive_all.at[row])

    def first(s, value):
        u0[s] = -value

    to_bonds(lambda l: drive_all[l // cells_dev, lax.rem(l, cells_dev)], first)

    def row_block(peer):
        return pl.ds(pl.multiple_of(peer * block, block), block)

    def operate(n, u, u_next, beside, between):
        base = 1 + 4 * n
        to_charges(n, u)
        copies = send_row(base, lambda peer: charge_part.at[n, row_block(peer)], charge_in.at[n, r])
        charge_in[n, r] = charge_part[n, row_block(r), :]
        if beside is not None:
            beside()
        arrive(copies)
        own = charge_in[n, 0]
        for k in range(1, rows):
            own = own + charge_in[n, k]
        col_charge[n, r] = own
        row_charge[n, c] = own
        side = send_col(2 * n, lambda peer: row_charge.at[n, c], row_charge.at[n, c])
        copies = send_row(base + 1, lambda peer: col_charge.at[n, r], col_charge.at[n, r])
        between()
        arrive(side)
        for k in range(cols):
            for l in range(cells_dev):
                high, low = halves(row_charge[n, k, l * sets : (l + 1) * sets, :])
                row_parts[k * cells_dev + l, 0:sets, :] = high
                row_parts[k * cells_dev + l, sets : 2 * sets, :] = low

        def forward(k, t, cell):
            both = dot(row_parts[cell], tile_parts[t], NT)
            return both[0:sets, 0:lanes] + (
                both[sets : 2 * sets, 0:lanes] + both[0:sets, lanes : 2 * lanes]
            )

        add_slots(0, tile_slots, group_cells, forward, products, pot_part.at[n])
        parts = send_row(base + 2, lambda peer: pot_part.at[n, row_block(peer)], pot_in.at[n, r])
        pot_in[n, r] = pot_part[n, row_block(r), :]
        arrive(copies)
        for k in range(rows):
            for l in range(cells_dev):
                high, low = halves(col_charge[n, k, l * sets : (l + 1) * sets, :])
                place = k * cells_dev + l
                col_parts[place, 0:sets, 0:lanes] = high
                col_parts[place, 0:sets, lanes : 2 * lanes] = high
                col_parts[place, sets : 2 * sets, 0:lanes] = low
                col_parts[place, sets : 2 * sets, lanes : 2 * lanes] = jnp.zeros_like(low)

        def backward(k, t, cell):
            both = dot(col_parts[cell], tile_parts[t])
            return both[0:sets] + both[sets : 2 * sets]

        add_slots(1, tile_slots, row_cells, backward, products, mirror_part.at[n])
        side = send_col(2 * n + 1, lambda peer: mirror_part.at[n, row_block(peer)], mirror_in.at[n, c])
        mirror_in[n, c] = mirror_part[n, row_block(c), :]
        arrive(parts)
        total = pot_in[n, 0]
        for k in range(1, rows):
            total = total + pot_in[n, k]
        arrive(side)
        for k in range(cols):
            total = total + mirror_in[n, k]
        own = col_charge[n, r]
        for l in range(cells_dev):
            part = slice(l * sets, (l + 1) * sets)
            pot_all[n, r, part, :] = total[part] + hardness[l : l + 1, :] * own[part]
        copies = gather_begin(base + 3, pot_all.at[n, r], lambda row: pot_all.at[n, row])
        gather_end(base + 3, copies, lambda row: pot_all.at[n, row])

        def update(s, value):
            u_next[s] = value + stiffness[pl.ds(table[20, s], 1), :] * u[s]

        to_bonds(lambda l: pot_all[n, l // cells_dev, pl.ds(pl.multiple_of(lax.rem(l, cells_dev) * sets, sets), sets), :], update)

    def pair_sums(pair):
        def body(s, sums):
            a, b = pair(s)
            return sums[0] + a, sums[1] + b

        zero = jnp.zeros((sets, lanes), jnp.float32)
        a, b = lax.fori_loop(0, link_slots, body, (zero, zero))
        a = jnp.sum(a, axis=1, keepdims=True)
        b = jnp.sum(b, axis=1, keepdims=True)
        lane = lax.broadcasted_iota(jnp.int32, (sets, lanes), 1)
        return jnp.where(lane == 0, a, jnp.where(lane == 1, b, 0.0))

    def dots_begin(n, values):
        dots_row[n, r] = values
        return send_row(9 + n, lambda peer: dots_row.at[n, r], dots_row.at[n, r])

    def dots_middle(n, copies):
        arrive(copies)
        total = dots_row[n, 0]
        for k in range(1, rows):
            total = total + dots_row[n, k]
        dots_col[n, c] = total
        return send_col(7 + n, lambda peer: dots_col.at[n, c], dots_col.at[n, c])

    def dots_end(n, copies):
        arrive(copies)
        total = dots_col[n, 0]
        for k in range(1, cols):
            total = total + dots_col[n, k]
        return total[:, 0:1], total[:, 1:2]

    bond_copies = {}

    def prepare_tiles():
        bond_copies[0] = send_bonds(0, u0)
        for i in range(chunks):
            tile_copies[i].wait()
            lax.fori_loop(i * per_chunk, (i + 1) * per_chunk, split_tiles, 0)

    operate(0, u0, u1, prepare_tiles, lambda: None)

    state = {}

    def first_sums():
        state["copies"] = dots_begin(0, pair_sums(lambda s: (u0[s] * u0[s], u0[s] * u1[s])))
        bond_copies[1] = send_bonds(1, u1)

    def second_sums():
        state["copies"] = dots_middle(0, state["copies"])

    operate(1, u1, u2, first_sums, second_sums)
    norm0, energy0 = dots_end(0, state["copies"])
    step0 = norm0 / energy0

    def last_pair(s):
        one = u1[s]
        residual = u0[s] - step0 * one
        applied = one - step0 * u2[s]
        return residual * residual, residual * applied

    copies = dots_begin(1, pair_sums(last_pair))
    bond_copies[2] = send_bonds(2, u2)
    copies = dots_middle(1, copies)
    for n in range(3):
        arrive(bond_copies[n])
    norm1, energy1 = dots_end(1, copies)
    gain = norm1 / norm0
    step1 = norm1 / (energy1 - gain * norm1 / step0)
    for j in range(share):
        part = slice(j * sets, (j + 1) * sets)
        total = []
        for n in range(3):
            value = bond_in[n, 0, part, :]
            for k in range(1, cols):
                value = value + bond_in[n, k, part, :]
            total.append(value)
        residual = total[0] - step0 * total[1]
        applied = total[1] - step0 * total[2]
        out_solution[j] = step0 * total[0] + step1 * (residual + gain * total[0])
        out_residual[j] = residual - step1 * (applied + gain * total[1])
    for copy in started:
        copy.wait_send()


def on_device(
    charge_drive,
    hardness,
    bond_stiffness,
    coulomb_tiles,
    tile_rows,
    tile_cols,
    tile_count,
    link_bonds,
    link_cells,
    link_ends,
    link_carry,
    link_count,
):
    rows, cols = lax.axis_size("row"), lax.axis_size("col")
    cells_dev, sets, lanes = charge_drive.shape
    tile_slots, link_slots = coulomb_tiles.shape[0], link_bonds.shape[0]
    row_bonds = bond_stiffness.shape[0]
    group_cells, row_cells = rows * cells_dev, cols * cells_dev
    share = row_bonds // cols
    block = cells_dev * sets
    f32, bf16 = jnp.float32, jnp.bfloat16
    vmem = pl.BlockSpec(memory_space=pltpu.VMEM)
    width = -(-max(tile_slots, link_slots, group_cells, row_bonds) // 128) * 128
    hbm = pl.BlockSpec(memory_space=pltpu.HBM)
    table = pl.pallas_call(
        order_kernel,
        out_shape=jax.ShapeDtypeStruct((24, width), jnp.int32),
        in_specs=[hbm] * 2 + [vmem] * 2 + [pl.BlockSpec(memory_space=pltpu.SMEM)] * 2,
        out_specs=vmem,
        scratch_shapes=[
            pltpu.VMEM((8, width), jnp.int32),
            pltpu.SemaphoreType.DMA((2,)),
        ],
        compiler_params=pltpu.CompilerParams(vmem_limit_bytes=67043328),
    )(
        tile_rows.reshape(1, -1), tile_cols.reshape(1, -1), link_bonds.reshape(1, -1), link_cells.reshape(1, -1),
        tile_count, link_count,
    )
    out = jax.ShapeDtypeStruct((share, sets, lanes), f32)
    sizes = (cells_dev, sets, lanes, tile_slots, link_slots, row_bonds)
    chunks = 8
    return pl.pallas_call(
        functools.partial(kernel, rows, cols, sizes),
        out_shape=(out, out),
        in_specs=[pl.BlockSpec(memory_space=pltpu.SMEM)] + [hbm] * 6,
        out_specs=(vmem, vmem),
        scratch_shapes=[
            pltpu.VMEM(hardness.shape, f32),
            pltpu.VMEM(bond_stiffness.shape, f32),
            pltpu.VMEM(link_ends.shape, jnp.int32),
            pltpu.VMEM(link_carry.shape, jnp.int32),
            pltpu.VMEM((tile_slots, lanes, lanes), f32),
            pltpu.VMEM((tile_slots, 2 * lanes, lanes), bf16),
            pltpu.VMEM((link_slots, lanes, lanes), bf16),
            pltpu.VMEM((link_slots, sets, lanes), f32),
            pltpu.VMEM((link_slots, sets, lanes), f32),
            pltpu.VMEM((link_slots, sets, lanes), f32),
            pltpu.VMEM((tile_slots, sets, lanes), f32),
            pltpu.VMEM((link_slots, sets, lanes), f32),
            pltpu.VMEM((link_slots, sets, lanes), f32),
            pltpu.VMEM((rows, cells_dev, sets, lanes), f32),
            pltpu.VMEM((2, group_cells * sets, lanes), f32),
            pltpu.VMEM((2, rows, block, lanes), f32),
            pltpu.VMEM((2, cols, block, lanes), f32),
            pltpu.VMEM((2, rows, block, lanes), f32),
            pltpu.VMEM((row_cells, 2 * sets, lanes), bf16),
            pltpu.VMEM((group_cells, 2 * sets, 2 * lanes), bf16),
            pltpu.VMEM((2, group_cells * sets, lanes), f32),
            pltpu.VMEM((2, rows, block, lanes), f32),
            pltpu.VMEM((2, row_cells * sets, lanes), f32),
            pltpu.VMEM((2, cols, block, lanes), f32),
            pltpu.VMEM((2, rows, block, lanes), f32),
            pltpu.VMEM((group_cells, 2 * sets, lanes), bf16),
            pltpu.VMEM((3, row_bonds * sets, lanes), f32),
            pltpu.VMEM((3, cols, share * sets, lanes), f32),
            pltpu.VMEM((2, rows, sets, lanes), f32),
            pltpu.VMEM((2, cols, sets, lanes), f32),
            pltpu.SemaphoreType.DMA((5,)),
            pltpu.SemaphoreType.DMA((chunks,)),
            pltpu.SemaphoreType.DMA((11, rows)),
            pltpu.SemaphoreType.DMA((11, rows)),
            pltpu.SemaphoreType.DMA((9, cols)),
            pltpu.SemaphoreType.DMA((9, cols)),
        ],
        compiler_params=pltpu.CompilerParams(
            collective_id=0, has_side_effects=True, vmem_limit_bytes=67043328
        ),
    )(
        table, charge_drive, hardness, bond_stiffness, coulomb_tiles, link_ends, link_carry,
    )


def solution(mesh):
    return jax.shard_map(
        on_device,
        mesh=mesh,
        in_specs=(
            P(("row", "col"), None, None),
            P(("row", "col"), None),
            P("row", None),
            P(("row", "col"), None, None),
            P(("row", "col")),
            P(("row", "col")),
            P(("row", "col")),
            P(("row", "col")),
            P(("row", "col")),
            P(("row", "col"), None, None),
            P(("row", "col"), None),
            P(("row", "col")),
        ),
        out_specs=(P(("row", "col"), None, None), P(("row", "col"), None, None)),
        check_vma=False,
    )
```

profile of v0, /device:TPU:1, one launch (start us, length us, event | category | flops | bytes accessed | tf_op | source)
XLA Modules:
  0.0 96.9 jit_solution(1025959246330363016)
XLA Ops:
  1.9 2.8 %shard_map.131.table = s32[24,128]{1,0:T(8,128)} custom-call(s32[1,128]{1,0:T(1,128)} %bitcast.4, s32[1,128]{1,0:T(1,128)} %bitcast.5, s32[1,32]{1,0:T(1,128)} %bitcast.6, s32[1,32]{1,0:T(1,128)} %bitcast.7, s32[1]{0:T(128)S(6)} %copy.16.tiles_live, s32[1]{0:T(128)S(6)} %copy.17.links_live), custom_call_target="tpu_custom_call" | custom-call | tf_op jit(solution)/shard_map/pallas_call | solution.py:457
  4.7 89.2 %shard_map.132 = (f32[8,16,128]{2,1,0:T(8,128)}, f32[8,16,128]{2,1,0:T(8,128)}) custom-call(s32[24,128]{1,0:T(8,128)} %shard_map.131.table, f32[4,16,128]{2,1,0:T(8,128)} %drive.1, f32[4,128]{1,0:T(4,128)} %hardness_hbm.1, f32[32,128]{1,0:T(8,128)} %stiffness_hbm.1, f32[128,128,128]{2,1,0:T(8,128)} %tiles_hbm.1, s32[32,2,128]{2,1,0:T(2,128)} %ends_hbm.1, ...), custom_call_target="tpu_custom_call" | custom-call | tf_op jit(solution)/shard_map/pallas_call | solution.py:474
  93.9 1.5 %copy.18 = f32[8,16,128]{2,1,0:T(8,128)} copy(f32[8,16,128]{2,1,0:T(8,128)} %get-tuple-element.4) | data formatting | bytes 131072
  95.4 1.5 %copy.19 = f32[8,16,128]{2,1,0:T(8,128)} copy(f32[8,16,128]{2,1,0:T(8,128)} %get-tuple-element.5) | data formatting | bytes 131072
where the time goes:
time: 97.5 us; the launch traced here: 96.9 us
  Pallas kernels  92 us (94%)
  local copies, waits for them, and re-layouts  2.95 us (3%)
  between operations  1.94 us (2%)
    pallas_call x1, Pallas kernels, on_device(): pl.pallas_call(functools.partial(kernel, rows, cols, sizes), out_shape=(o...  89.2 us
    unnamed x2, local copies, waits for them, and re-layouts  2.95 us
    pallas_call x1, Pallas kernels, on_device(): pl.pallas_call(order_kernel, out_shape=jax.ShapeDtypeStruct((24, width),...  2.79 us

commit v1 on v0

v1 whole, which is shorter than its diff:
```python
import functools

import jax
import jax.numpy as jnp
from jax import lax
from jax.experimental import pallas as pl
from jax.experimental.pallas import tpu as pltpu
from jax.sharding import PartitionSpec as P

MESH = pl.DeviceIdType.MESH
NT = (((1,), (1,)), ((), ()))
NN = (((1,), (0,)), ((), ()))


def halves(value):
    high = value.astype(jnp.bfloat16)
    low = (value - high.astype(jnp.float32)).astype(jnp.bfloat16)
    return high, low


def dot(left, right, dims=NN):
    return lax.dot_general(left, right, dims, preferred_element_type=jnp.float32)


class Row:
    def __init__(self, rows, send, recv, started):
        self.rows, self.send, self.recv, self.started = rows, send, recv, started
        self.inner = 2 if rows % 2 == 0 else 1
        self.outer = rows // self.inner
        self.r, self.c = lax.axis_index("row"), lax.axis_index("col")
        self.high, self.low = self.r // self.inner, lax.rem(self.r, self.inner)

    def copy(self, phase, index, source, target, peer):
        copy = pltpu.make_async_remote_copy(
            src_ref=source, dst_ref=target,
            send_sem=self.send.at[phase, index], recv_sem=self.recv.at[phase, index],
            device_id=(peer, self.c), device_id_type=MESH,
        )
        copy.start()
        self.started.append(copy)
        return copy

    def near_peer(self):
        return self.high * self.inner + self.inner - 1 - self.low

    def gather_begin(self, phase, source, slot_of):
        far = [
            self.copy(
                phase, k * self.inner, source, slot_of(self.r),
                lax.rem(self.high + k, self.outer) * self.inner + self.low,
            )
            for k in range(1, self.outer)
        ]
        near = [
            self.copy(phase, 1, source, slot_of(self.r), self.near_peer())
            for _ in range(self.inner - 1)
        ]
        return far, near

    def gather_relay(self, phase, copies, slot_of):
        far, near = copies
        for k, copy in enumerate(far, 1):
            copy.wait_recv()
            if self.inner > 1:
                block = slot_of(lax.rem(self.high + self.outer - k, self.outer) * self.inner + self.low)
                near.append(self.copy(phase, k * self.inner + 1, block, block, self.near_peer()))

    def gather_end(self, copies):
        for copy in copies[1]:
            copy.wait_recv()


def greet(rows, cols, r, c, with_cols):
    barrier = pltpu.get_barrier_semaphore()
    for k in range(1, rows):
        pl.semaphore_signal(barrier, inc=1, device_id=(lax.rem(r + k, rows), c), device_id_type=MESH)
    if with_cols:
        for k in range(1, cols):
            pl.semaphore_signal(barrier, inc=1, device_id=(r, lax.rem(c + k, cols)), device_id_type=MESH)
    return barrier


def link_kernel(
    rows, cols, sizes,
    tile_rows, tile_cols, link_bonds, link_cells, tiles_live, links_live, bonds, ends_hbm, carry, stiffness,
    table, ends_all, weight_all, cells_all,
    ids, sem, row_send, row_recv,
):
    link_slots, lanes = carry.shape
    width = ids.shape[1]
    started = []
    row = Row(rows, row_send, row_recv, started)
    r, c = row.r, row.c
    barrier = greet(rows, cols, r, c, False)
    own_ends = pltpu.make_async_copy(ends_hbm, ends_all.at[r], sem.at[2])
    own_ends.start()
    ids[...] = jnp.zeros_like(ids)
    copies = []
    for i, (source, target) in enumerate((
        (tile_rows, ids.at[0:1, 0 : tile_rows.shape[1]]), (tile_cols, ids.at[1:2, 0 : tile_cols.shape[1]]),
    )):
        copy = pltpu.make_async_copy(source, target, sem.at[i])
        copy.start()
        copies.append(copy)
    ids[2:3, 0:link_slots] = link_bonds[...]
    ids[3:4, 0:link_slots] = link_cells[...]
    tile_count, link_count = tiles_live[0], links_live[0]
    slot = lax.broadcasted_iota(jnp.int32, (8, width), 1)
    cells_all[r] = jnp.where(slot < link_count, jnp.broadcast_to(ids[3:4, :], (8, width)), -1)
    for s in range(link_slots):
        live = jnp.full((1, lanes), s, jnp.int32) < link_count
        kept = jnp.where(live, carry[s : s + 1, :], 0).astype(jnp.float32)
        weight_all[r, s : s + 1, :] = kept * stiffness[pl.ds(bonds[0, s], 1), :]
    slots = (lambda i: ends_all.at[i]), (lambda i: weight_all.at[i]), (lambda i: cells_all.at[i])
    pl.semaphore_wait(barrier, rows - 1)
    gathers = [
        row.gather_begin(phase, ends_hbm if phase == 0 else of(r), of) for phase, of in enumerate(slots)
    ]
    for copy in copies:
        copy.wait()
    beyond = 1 << 20
    down = lax.broadcasted_iota(jnp.int32, (width, width), 0)
    across = lax.broadcasted_iota(jnp.int32, (width, width), 1)

    def total(value, axis):
        return jnp.sum(value, axis=axis, keepdims=True)

    def column(value):
        return total(jnp.where(down == across, value, 0), 1)

    for place, (key_row, other, count) in enumerate((
        (0, 1, tile_count), (1, 0, tile_count), (3, 3, link_count), (2, 2, link_count),
    )):
        key = jnp.where(across[0:1] < count, ids[key_row : key_row + 1, :], beyond)
        mine = column(key)
        equal_before = total(jnp.where((key == mine) & (across < down), 1, 0), 1)
        rank = total(jnp.where(key < mine, 1, 0), 1) + equal_before
        here = rank == across
        upto = total(jnp.where(mine <= across, 1, 0), 0)
        fewer = total(jnp.where(mine < across, 1, 0), 0)
        at = 5 * place
        table[at : at + 1, :] = total(jnp.where(here, down, 0), 0)
        table[at + 1 : at + 2, :] = total(jnp.where(here & (equal_before > 0), 1, 0), 0)
        table[at + 2 : at + 3, :] = jnp.maximum(upto - 1, 0)
        table[at + 3 : at + 4, :] = jnp.where(upto > fewer, 1, 0)
        table[at + 4 : at + 5, :] = total(jnp.where(here, column(ids[other : other + 1, :]), 0), 0)
    table[20:22, :] = ids[2:4, :]
    table[22:24, :] = jnp.full((2, width), link_count, jnp.int32)
    own_ends.wait()
    for phase, of in enumerate(slots):
        row.gather_relay(phase, gathers[phase], of)
    for gather in gathers:
        row.gather_end(gather)
    for copy in started:
        copy.wait_send()


GROUP = 4


def cell_kernel(
    rows, sizes, cells, ends_all, weight_all, drive, square_out, charge_out, fixed_out, sums_out, listed, acc,
):
    cells_dev, sets, lanes, link_slots = sizes
    first = lax.axis_index("row") * cells_dev
    acc[...] = jnp.zeros_like(acc)

    def collect(i, found):
        for s in range(link_slots):
            local = cells[i, s] - first
            listed[found] = (i * link_slots + s) * cells_dev + local
            found = found + jnp.where((local >= 0) & (local < cells_dev), 1, 0)
        return found

    found = lax.fori_loop(0, rows, collect, jnp.int32(0))
    for e in range(GROUP):
        listed[found + e] = 0
    atom = lax.broadcasted_iota(jnp.int32, (lanes, lanes), 0)

    def visit(g, sums):
        norm, energy = sums
        for e in range(GROUP):
            i = g * GROUP + e
            code = listed[i]
            s, l = code // cells_dev, lax.rem(code, cells_dev)
            real = jnp.full((1, lanes), i, jnp.int32) < found
            pair = ends_all[s]
            weight = jnp.where(real, weight_all[pl.ds(s, 1), :], 0.0)
            kept = jnp.where(weight != 0.0, 1.0, 0.0)
            gain = jnp.where(atom == pair[0:1, :], kept, 0.0)
            lose = jnp.where(atom == pair[1:2, :], kept, 0.0)
            matrix = (gain - lose).astype(jnp.bfloat16)
            high, low = halves(drive[l])
            both = dot(jnp.concatenate([high, low], axis=0), matrix)
            u = -(both[0:sets] + both[sets : 2 * sets])
            ku = weight * u
            norm = norm + u * u
            energy = energy + ku * u
            left = jnp.concatenate([matrix, *halves(u), *halves(ku)], axis=0)
            acc[l] += dot(left, matrix, NT)
        return norm, energy

    zero = jnp.zeros((sets, lanes), jnp.float32)
    norm, energy = lax.fori_loop(0, (found + GROUP - 1) // GROUP, visit, (zero, zero))
    sums_out[0] = norm
    sums_out[1] = energy
    for l in range(cells_dev):
        high, low = halves(acc[l, 0:lanes, :])
        square_out[l, :, 0:lanes] = high
        square_out[l, :, lanes : 2 * lanes] = low
        at = lanes
        charge_out[l] = acc[l, at : at + sets, :] + acc[l, at + sets : at + 2 * sets, :]
        at = lanes + 2 * sets
        fixed_out[l] = acc[l, at : at + sets, :] + acc[l, at + sets : at + 2 * sets, :]


def kernel(
    rows, cols, sizes,
    table, drive, hardness_hbm, stiffness_hbm, tiles_hbm, ends_hbm, carry_hbm, square, charge0, fixed, sums0,
    out_solution, out_residual,
    hardness, stiffness, ends, carry,
    tiles, tile_parts, incidence, u0, u1, u2, products, bond_products,
    drive_all, row_charge, col_charge,
    row_parts, col_parts, pot_part, pot_in, mirror_part, mirror_in, pot_all, pot_parts,
    bond_part, bond_in, dots_row, dots_col,
    small_sem, tile_sem, row_send, row_recv, col_send, col_recv,
):
    cells_dev, sets, lanes, tile_slots, link_slots, row_bonds = sizes
    group_cells, row_cells = rows * cells_dev, cols * cells_dev
    share = row_bonds // cols
    block = cells_dev * sets
    started = []
    row = Row(rows, row_send, row_recv, started)
    r, c = row.r, row.c

    small = []
    for i, (source, target) in enumerate((
        (ends_hbm, ends), (carry_hbm, carry),
        (hardness_hbm, hardness), (stiffness_hbm, stiffness), (drive, drive_all.at[r]),
    )):
        copy = pltpu.make_async_copy(source, target, small_sem.at[i])
        copy.start()
        small.append(copy)
    barrier = greet(rows, cols, r, c, True)
    chunks = tile_sem.shape[0]
    per_chunk = tile_slots // chunks
    tile_copies = []
    for i in range(chunks):
        part = pl.ds(i * per_chunk, per_chunk)
        copy = pltpu.make_async_copy(tiles_hbm.at[part], tiles.at[part], tile_sem.at[i])
        copy.start()
        tile_copies.append(copy)
    for l in range(cells_dev):
        part = slice(l * sets, (l + 1) * sets)
        col_charge[0, r, part, :] = charge0[l]
        row_charge[0, c, part, :] = charge0[l]
    link_count = table[22, 0]
    small[0].wait()
    small[1].wait()

    def build_incidence(s, _):
        atom = lax.broadcasted_iota(jnp.int32, (lanes, lanes), 0)
        pair = ends[s]
        live = jnp.full((1, lanes), s, jnp.int32) < link_count
        kept = jnp.where(live, carry[pl.ds(s, 1), :], 0).astype(jnp.float32)
        gain = jnp.where(atom == pair[0:1, :], kept, 0.0)
        lose = jnp.where(atom == pair[1:2, :], kept, 0.0)
        incidence[s] = (gain - lose).astype(jnp.bfloat16)
        return 0

    lax.fori_loop(0, link_slots, build_incidence, 0)
    pl.semaphore_wait(barrier, rows + cols - 2)

    def send_row(phase, source, target):
        return [
            row.copy(phase, k, source(lax.rem(r + k, rows)), target, lax.rem(r + k, rows))
            for k in range(1, rows)
        ]

    def send_col(phase, source, target):
        copies = []
        for k in range(1, cols):
            peer = lax.rem(c + k, cols)
            copy = pltpu.make_async_remote_copy(
                src_ref=source(peer), dst_ref=target,
                send_sem=col_send.at[phase, k], recv_sem=col_recv.at[phase, k],
                device_id=(r, peer), device_id_type=MESH,
            )
            copy.start()
            copies.append(copy)
        started.extend(copies)
        return copies

    def arrive(copies):
        for copy in copies:
            copy.wait_recv()

    def split_tiles(t, _):
        high, low = halves(tiles[t])
        tile_parts[t, 0:lanes, :] = high
        tile_parts[t, lanes : 2 * lanes, :] = low
        return 0

    UNROLL = 32

    def slot(s):
        return pl.ds(pl.multiple_of(s * sets, sets), sets)

    def add_slots(place, value, running, carried, start, stop):
        def body(i, carried):
            for j in range(UNROLL):
                k = i * UNROLL + j
                kept = jnp.full((sets, lanes), table[5 * place + 1, k], jnp.int32).astype(jnp.float32)
                carried = carried * kept + value(k, table[5 * place, k], table[5 * place + 4, k])
                running[k] = carried
            return carried

        return lax.fori_loop(start // UNROLL, stop // UNROLL, body, carried)

    def spread_slots(place, size, running, target):
        def spread(i, _):
            for j in range(4):
                l = i * 4 + j
                some = jnp.full((sets, lanes), table[5 * place + 3, l], jnp.int32).astype(jnp.float32)
                found = running[table[5 * place + 2, l]]
                target[slot(l), :] = found * some
            return 0

        lax.fori_loop(0, size // 4, spread, 0)

    nothing = jnp.zeros((sets, lanes), jnp.float32)

    def to_bonds(potential_of, update):
        def fill(l, _):
            high, low = halves(potential_of(l))
            pot_parts[l, 0:sets, :] = high
            pot_parts[l, sets : 2 * sets, :] = low
            return 0

        lax.fori_loop(0, group_cells, fill, 0)

        def body(i, _):
            for j in range(UNROLL):
                s = i * UNROLL + j
                both = dot(pot_parts[table[21, s]], incidence[s])
                update(s, both[0:sets] + both[sets : 2 * sets])
            return 0

        lax.fori_loop(0, link_slots // UNROLL, body, 0)

    def send_bonds(n, u):
        add_slots(3, lambda k, s, _: u[s], bond_products, nothing, 0, link_slots)
        spread_slots(3, row_bonds, bond_products, bond_part.at[n])
        size = share * sets
        copies = send_col(
            4 + n,
            lambda peer: bond_part.at[n, pl.ds(pl.multiple_of(peer * size, size), size)],
            bond_in.at[n, c],
        )
        bond_in[n, c] = bond_part[n, pl.ds(pl.multiple_of(c * size, size), size), :]
        return copies

    def row_block(peer):
        return pl.ds(pl.multiple_of(peer * block, block), block)

    def drive_slot(i):
        return drive_all.at[i]

    def operate(n, background, prepare, middle, slack):
        def charge_slot(i):
            return col_charge.at[n, i]

        side = send_col(n, lambda peer: row_charge.at[n, c], row_charge.at[n, c])
        gather = row.gather_begin(3 * n, col_charge.at[n, r], charge_slot)
        copies, other_slot, phase = background()
        prepare()
        arrive(side)
        for k in range(cols):
            for l in range(cells_dev):
                high, low = halves(row_charge[n, k, l * sets : (l + 1) * sets, :])
                row_parts[k * cells_dev + l, 0:sets, :] = high
                row_parts[k * cells_dev + l, sets : 2 * sets, :] = low

        def forward(k, t, cell):
            both = dot(row_parts[cell], tile_parts[t], NT)
            return both[0:sets, 0:lanes] + (
                both[sets : 2 * sets, 0:lanes] + both[0:sets, lanes : 2 * lanes]
            )

        half = tile_slots // (2 * UNROLL) * UNROLL
        carried = add_slots(0, forward, products, nothing, 0, half)
        row.gather_relay(3 * n, gather, charge_slot)
        add_slots(0, forward, products, carried, half, tile_slots)
        spread_slots(0, group_cells, products, pot_part.at[n])
        parts = send_row(3 * n + 1, lambda peer: pot_part.at[n, row_block(peer)], pot_in.at[n, r])
        pot_in[n, r] = pot_part[n, row_block(r), :]
        row.gather_relay(phase, copies, other_slot)
        middle()
        row.gather_end(gather)
        for k in range(rows):
            for l in range(cells_dev):
                high, low = halves(col_charge[n, k, l * sets : (l + 1) * sets, :])
                place = k * cells_dev + l
                col_parts[place, 0:sets, 0:lanes] = high
                col_parts[place, 0:sets, lanes : 2 * lanes] = high
                col_parts[place, sets : 2 * sets, 0:lanes] = low
                col_parts[place, sets : 2 * sets, lanes : 2 * lanes] = jnp.zeros_like(low)

        def backward(k, t, cell):
            both = dot(col_parts[cell], tile_parts[t])
            return both[0:sets] + both[sets : 2 * sets]

        add_slots(1, backward, products, nothing, 0, tile_slots)
        spread_slots(1, row_cells, products, mirror_part.at[n])
        side = send_col(2 + n, lambda peer: mirror_part.at[n, row_block(peer)], mirror_in.at[n, c])
        mirror_in[n, c] = mirror_part[n, row_block(c), :]
        row.gather_end(copies)
        slack()
        arrive(parts)
        total = pot_in[n, 0]
        for k in range(1, rows):
            total = total + pot_in[n, k]
        arrive(side)
        for k in range(cols):
            total = total + mirror_in[n, k]
        own = col_charge[n, r]
        for l in range(cells_dev):
            part = slice(l * sets, (l + 1) * sets)
            pot_all[n, r, part, :] = total[part] + hardness[l : l + 1, :] * own[part]

    def pot_slot(n):
        return lambda i: pot_all.at[n, i]

    def potential(n):
        return lambda l: pot_all[
            n, l // cells_dev, pl.ds(pl.multiple_of(lax.rem(l, cells_dev) * sets, sets), sets), :
        ]

    def own_cells(n, l):
        part = slice(l * sets, (l + 1) * sets)
        return col_charge[n, r, part, :], pot_all[n, r, part, :]

    def packed(a, b):
        a = jnp.sum(a, axis=1, keepdims=True)
        b = jnp.sum(b, axis=1, keepdims=True)
        lane = lax.broadcasted_iota(jnp.int32, (sets, lanes), 1)
        return jnp.where(lane == 0, a, jnp.where(lane == 1, b, 0.0))

    def dots_begin(n, values):
        dots_row[n, r] = values
        return send_row(7 + n, lambda peer: dots_row.at[n, r], dots_row.at[n, r])

    def dots_middle(n, copies):
        arrive(copies)
        total = dots_row[n, 0]
        for k in range(1, rows):
            total = total + dots_row[n, k]
        dots_col[n, c] = total
        return send_col(7 + n, lambda peer: dots_col.at[n, c], dots_col.at[n, c])

    def dots_end(n, copies):
        arrive(copies)
        total = dots_col[n, 0]
        for k in range(1, cols):
            total = total + dots_col[n, k]
        return total[:, 0:1], total[:, 1:2]

    state = {}

    def drive_background():
        return row.gather_begin(2, drive, drive_slot), drive_slot, 2

    def prepare_tiles():
        for copy in small[2:]:
            copy.wait()
        for i in range(chunks):
            tile_copies[i].wait()
            lax.fori_loop(i * per_chunk, (i + 1) * per_chunk, split_tiles, 0)

    def first_bonds():
        def first(s, value):
            u0[s] = -value

        to_bonds(lambda l: drive_all[l // cells_dev, lax.rem(l, cells_dev)], first)
        state["bonds0"] = send_bonds(0, u0)

    operate(0, drive_background, prepare_tiles, lambda: None, first_bonds)

    energy = sums0[1]
    for l in range(cells_dev):
        part = slice(l * sets, (l + 1) * sets)
        charge, value = own_cells(0, l)
        both = dot(jnp.concatenate(halves(value), axis=0), square[l])
        new = both[0:sets, 0:lanes] + (
            both[sets : 2 * sets, 0:lanes] + both[0:sets, lanes : 2 * lanes]
        )
        new = new + fixed[l]
        col_charge[1, r, part, :] = new
        row_charge[1, c, part, :] = new
        energy = energy + charge * value

    def potential_background():
        gather = row.gather_begin(5, pot_all.at[0, r], pot_slot(0))
        state["dots"] = dots_begin(0, packed(sums0[0], energy))
        return gather, pot_slot(0), 5

    def first_dots():
        state["dots"] = dots_middle(0, state["dots"])

    def second_bonds():
        def update(s, value):
            u1[s] = value + stiffness[pl.ds(table[20, s], 1), :] * u0[s]

        to_bonds(potential(0), update)
        state["bonds1"] = send_bonds(1, u1)
        norm, energy = dots_end(0, state["dots"])
        state["norm"], state["step"] = norm, norm / energy

        def body(i, sums):
            a, b = sums
            for j in range(4):
                s = i * 4 + j
                residual = u0[s] - state["step"] * u1[s]
                square_of = residual * residual
                a = a + square_of
                b = b + stiffness[pl.ds(table[20, s], 1), :] * square_of
            return a, b

        state["sums"] = lax.fori_loop(0, link_slots // 4, body, (nothing, nothing))

    operate(1, potential_background, lambda: None, first_dots, second_bonds)
    gather = row.gather_begin(6, pot_all.at[1, r], pot_slot(1))
    norm0, step0 = state["norm"], state["step"]
    norm_part, energy_part = state["sums"]
    for l in range(cells_dev):
        charge, value = own_cells(0, l)
        charge1, value1 = own_cells(1, l)
        energy_part = energy_part + (charge - step0 * charge1) * (value - step0 * value1)
    copies = dots_begin(1, packed(norm_part, energy_part))
    row.gather_relay(6, gather, pot_slot(1))
    copies = dots_middle(1, copies)
    row.gather_end(gather)

    def last(s, value):
        u2[s] = value + stiffness[pl.ds(table[20, s], 1), :] * u1[s]

    to_bonds(potential(1), last)
    bonds2 = send_bonds(2, u2)
    norm1, energy1 = dots_end(1, copies)
    arrive(state["bonds0"])
    arrive(state["bonds1"])
    arrive(bonds2)
    gain = norm1 / norm0
    step1 = norm1 / (energy1 - gain * norm1 / step0)
    for j in range(share):
        part = slice(j * sets, (j + 1) * sets)
        total = []
        for n in range(3):
            value = bond_in[n, 0, part, :]
            for k in range(1, cols):
                value = value + bond_in[n, k, part, :]
            total.append(value)
        residual = total[0] - step0 * total[1]
        applied = total[1] - step0 * total[2]
        out_solution[j] = step0 * total[0] + step1 * (residual + gain * total[0])
        out_residual[j] = residual - step1 * (applied + gain * total[1])
    for copy in started:
        copy.wait_send()


def on_device(
    charge_drive,
    hardness,
    bond_stiffness,
    coulomb_tiles,
    tile_rows,
    tile_cols,
    tile_count,
    link_bonds,
    link_cells,
    link_ends,
    link_carry,
    link_count,
):
    rows, cols = lax.axis_size("row"), lax.axis_size("col")
    cells_dev, sets, lanes = charge_drive.shape
    tile_slots, link_slots = coulomb_tiles.shape[0], link_bonds.shape[0]
    row_bonds = bond_stiffness.shape[0]
    group_cells, row_cells = rows * cells_dev, cols * cells_dev
    share = row_bonds // cols
    block = cells_dev * sets
    f32, bf16, i32 = jnp.float32, jnp.bfloat16, jnp.int32
    vmem = pl.BlockSpec(memory_space=pltpu.VMEM)
    smem = pl.BlockSpec(memory_space=pltpu.SMEM)
    hbm = pl.BlockSpec(memory_space=pltpu.HBM)
    width = -(-max(tile_slots, link_slots, group_cells, row_bonds) // 128) * 128
    bonds = link_bonds.reshape(1, -1)
    table, ends_all, weight_all, cells_all = pl.pallas_call(
        functools.partial(link_kernel, rows, cols, None),
        out_shape=(
            jax.ShapeDtypeStruct((24, width), i32),
            jax.ShapeDtypeStruct((rows, *link_ends.shape), i32),
            jax.ShapeDtypeStruct((rows, link_slots, lanes), f32),
            jax.ShapeDtypeStruct((rows, 8, width), i32),
        ),
        in_specs=[hbm] * 2 + [vmem] * 2 + [smem] * 3 + [hbm] + [vmem] * 2,
        out_specs=(vmem,) * 4,
        scratch_shapes=[
            pltpu.VMEM((8, width), i32),
            pltpu.SemaphoreType.DMA((3,)),
            pltpu.SemaphoreType.DMA((3, rows)),
            pltpu.SemaphoreType.DMA((3, rows)),
        ],
        compiler_params=pltpu.CompilerParams(
            collective_id=1, has_side_effects=True, vmem_limit_bytes=67043328
        ),
    )(
        tile_rows.reshape(1, -1), tile_cols.reshape(1, -1), bonds, link_cells.reshape(1, -1),
        tile_count, link_count, bonds, link_ends, link_carry, bond_stiffness,
    )
    square, charge0, fixed, sums0 = pl.pallas_call(
        functools.partial(cell_kernel, rows, (cells_dev, sets, lanes, link_slots)),
        out_shape=(
            jax.ShapeDtypeStruct((cells_dev, lanes, 2 * lanes), bf16),
            jax.ShapeDtypeStruct((cells_dev, sets, lanes), f32),
            jax.ShapeDtypeStruct((cells_dev, sets, lanes), f32),
            jax.ShapeDtypeStruct((2, sets, lanes), f32),
        ),
        in_specs=[smem] + [vmem] * 3,
        out_specs=(vmem,) * 4,
        scratch_shapes=[
            pltpu.SMEM((rows * link_slots + 2 * GROUP,), i32),
            pltpu.VMEM((cells_dev, lanes + 4 * sets, lanes), f32),
        ],
        compiler_params=pltpu.CompilerParams(vmem_limit_bytes=67043328),
    )(
        cells_all[:, 0, :], ends_all.reshape(rows * link_slots, *link_ends.shape[1:]),
        weight_all.reshape(rows * link_slots, lanes), charge_drive,
    )
    out = jax.ShapeDtypeStruct((share, sets, lanes), f32)
    sizes = (cells_dev, sets, lanes, tile_slots, link_slots, row_bonds)
    chunks = 8
    return pl.pallas_call(
        functools.partial(kernel, rows, cols, sizes),
        out_shape=(out, out),
        in_specs=[smem] + [hbm] * 6 + [vmem] * 4,
        out_specs=(vmem, vmem),
        scratch_shapes=[
            pltpu.VMEM(hardness.shape, f32),
            pltpu.VMEM(bond_stiffness.shape, f32),
            pltpu.VMEM(link_ends.shape, i32),
            pltpu.VMEM(link_carry.shape, i32),
            pltpu.VMEM((tile_slots, lanes, lanes), f32),
            pltpu.VMEM((tile_slots, 2 * lanes, lanes), bf16),
            pltpu.VMEM((link_slots, lanes, lanes), bf16),
            pltpu.VMEM((link_slots, sets, lanes), f32),
            pltpu.VMEM((link_slots, sets, lanes), f32),
            pltpu.VMEM((link_slots, sets, lanes), f32),
            pltpu.VMEM((tile_slots, sets, lanes), f32),
            pltpu.VMEM((link_slots, sets, lanes), f32),
            pltpu.VMEM((rows, cells_dev, sets, lanes), f32),
            pltpu.VMEM((2, cols, block, lanes), f32),
            pltpu.VMEM((2, rows, block, lanes), f32),
            pltpu.VMEM((row_cells, 2 * sets, lanes), bf16),
            pltpu.VMEM((group_cells, 2 * sets, 2 * lanes), bf16),
            pltpu.VMEM((2, group_cells * sets, lanes), f32),
            pltpu.VMEM((2, rows, block, lanes), f32),
            pltpu.VMEM((2, row_cells * sets, lanes), f32),
            pltpu.VMEM((2, cols, block, lanes), f32),
            pltpu.VMEM((2, rows, block, lanes), f32),
            pltpu.VMEM((group_cells, 2 * sets, lanes), bf16),
            pltpu.VMEM((3, row_bonds * sets, lanes), f32),
            pltpu.VMEM((3, cols, share * sets, lanes), f32),
            pltpu.VMEM((2, rows, sets, lanes), f32),
            pltpu.VMEM((2, cols, sets, lanes), f32),
            pltpu.SemaphoreType.DMA((5,)),
            pltpu.SemaphoreType.DMA((chunks,)),
            pltpu.SemaphoreType.DMA((9, rows)),
            pltpu.SemaphoreType.DMA((9, rows)),
            pltpu.SemaphoreType.DMA((9, cols)),
            pltpu.SemaphoreType.DMA((9, cols)),
        ],
        compiler_params=pltpu.CompilerParams(
            collective_id=0, has_side_effects=True, vmem_limit_bytes=67043328
        ),
    )(
        table, charge_drive, hardness, bond_stiffness, coulomb_tiles, link_ends, link_carry,
        square, charge0, fixed, sums0,
    )


def solution(mesh):
    return jax.shard_map(
        on_device,
        mesh=mesh,
        in_specs=(
            P(("row", "col"), None, None),
            P(("row", "col"), None),
            P("row", None),
            P(("row", "col"), None, None),
            P(("row", "col")),
            P(("row", "col")),
            P(("row", "col")),
            P(("row", "col")),
            P(("row", "col")),
            P(("row", "col"), None, None),
            P(("row", "col"), None),
            P(("row", "col")),
        ),
        out_specs=(P(("row", "col"), None, None), P(("row", "col"), None, None)),
        check_vma=False,
    )
```

time: 97.5 us -> 80.6 us (0.83)
  Pallas kernels: 92 us -> 74.4 us
  local copies, waits for them, and re-layouts: 2.95 us -> 4.31 us
    pallas_call x1, Pallas kernels: 89.2 us -> 55.4 us  [on_device(): pl.pallas_call(functools.partial(kernel, rows, cols, sizes), out_shape=(o...]
    pallas_call x1 -> x2, Pallas kernels: 2.79 us -> 19 us  [the longest x1 14.7 us: on_device(): pl.pallas_call(functools.partial(link_kernel, rows, cols, None), out_shap...]
where the time goes in v1:
time: 80.6 us; the launch traced here: 80.7 us
  Pallas kernels  74.4 us (92%)
  local copies, waits for them, and re-layouts  4.31 us (5%)
  between operations  1.94 us (2%)
    pallas_call x1, Pallas kernels, on_device(): pl.pallas_call(functools.partial(kernel, rows, cols, sizes), out_shape=(o...  55.4 us
    pallas_call x1, Pallas kernels, on_device(): pl.pallas_call(functools.partial(link_kernel, rows, cols, None), out_shap...  14.7 us
    pallas_call x1, Pallas kernels, on_device(): pl.pallas_call(functools.partial(cell_kernel, rows, (cells_dev, sets, lan...  4.29 us
    unnamed x2, local copies, waits for them, and re-layouts  2.95 us

profile of v1, /device:TPU:1, one launch (start us, length us, event | category | flops | bytes accessed | tf_op | source)
XLA Modules:
  0.0 80.7 jit_solution(6901229205184386465)
XLA Ops:
  1.9 14.7 %shard_map.131 = (s32[24,128]{1,0:T(8,128)}, s32[8,32,2,128]{3,2,1,0:T(2,128)}, f32[8,32,128]{2,1,0:T(8,128)}, s32[8,8,128]{2,1,0:T(8,128)}) custom-call(s32[1,128]{1,0:T(1,128)} %bitcast.12, s32[1,128]{1,0:T(1,128)} %bitcast.13, s32[1,32]{1,0:T(1,128)} %bitcast.10, s32[1,32]{1,0:T(1,128)} %bitcast.14, s32[1]{0:T(128)S(6)} %copy.17.tiles_live, ...), custom_call_target="tpu_custom_call" | custom-call | tf_op jit(solution)/shard_map/pallas_call | solution.py:598
  16.6 0.8 copy.14
  17.4 0.6 slice_bitcast_fusion.cells
  18.0 4.3 %shard_map.132 = (bf16[4,128,256]{2,1,0:T(8,128)(2,1)}, f32[4,16,128]{2,1,0:T(8,128)}, f32[4,16,128]{2,1,0:T(8,128)}, f32[2,16,128]{2,1,0:T(8,128)}) custom-call(s32[8,128]{1,0:T(8,128)} %slice_bitcast_fusion.cells, s32[256,2,128]{2,1,0:T(2,128)} %bitcast.8, f32[256,128]{1,0:T(8,128)} %bitcast.9, f32[4,16,128]{2,1,0:T(8,128)} %drive.3), custom_call_target="tpu_custom_call" | custom-call | tf_op jit(solution)/shard_map/pallas_call | solution.py:621
  22.3 55.4 %shard_map.133 = (f32[8,16,128]{2,1,0:T(8,128)}, f32[8,16,128]{2,1,0:T(8,128)}) custom-call(s32[24,128]{1,0:T(8,128)} %get-tuple-element.10.table, f32[4,16,128]{2,1,0:T(8,128)} %drive.3, f32[4,128]{1,0:T(4,128)} %hardness_hbm.1, f32[32,128]{1,0:T(8,128)} %stiffness_hbm.1, f32[128,128,128]{2,1,0:T(8,128)} %tiles_hbm.1, s32[32,2,128]{2,1,0:T(2,128)} %ends_hbm.3, ...), custom_call_target="tpu_custom_call" | custom-call | tf_op jit(solution)/shard_map/pallas_call | solution.py:643
  77.7 1.5 %copy.19 = f32[8,16,128]{2,1,0:T(8,128)} copy(f32[8,16,128]{2,1,0:T(8,128)} %get-tuple-element.20) | data formatting | bytes 131072
  79.2 1.5 %copy.20 = f32[8,16,128]{2,1,0:T(8,128)} copy(f32[8,16,128]{2,1,0:T(8,128)} %get-tuple-element.21) | data formatting | bytes 131072

commit v2 on v1

--- a/solution.py
+++ b/solution.py
@@ -40,15 +40,23 @@
         self.started.append(copy)
         return copy
 
+    def partner(self, k):
+        if self.outer & (self.outer - 1):
+            half = self.outer + k
+            return lax.rem(half - self.high, self.outer)
+        place, bit = self.high, 1
+        while bit < self.outer:
+            if k & bit:
+                place = place + bit - 2 * bit * lax.rem(self.high // bit, 2)
+            bit *= 2
+        return place
+
     def near_peer(self):
         return self.high * self.inner + self.inner - 1 - self.low
 
     def gather_begin(self, phase, source, slot_of):
         far = [
-            self.copy(
-                phase, k * self.inner, source, slot_of(self.r),
-                lax.rem(self.high + k, self.outer) * self.inner + self.low,
-            )
+            self.copy(phase, k * self.inner, source, slot_of(self.r), self.partner(k) * self.inner + self.low)
             for k in range(1, self.outer)
         ]
         near = [
@@ -57,12 +65,12 @@
         ]
         return far, near
 
-    def gather_relay(self, phase, copies, slot_of):
+    def gather_relay(self, phase, copies, slot_of, start=1, stop=None):
         far, near = copies
-        for k, copy in enumerate(far, 1):
-            copy.wait_recv()
+        for k in range(start, stop or self.outer):
+            far[k - 1].wait_recv()
             if self.inner > 1:
-                block = slot_of(lax.rem(self.high + self.outer - k, self.outer) * self.inner + self.low)
+                block = slot_of(self.partner(k) * self.inner + self.low)
                 near.append(self.copy(phase, k * self.inner + 1, block, block, self.near_peer()))
 
     def gather_end(self, copies):
@@ -82,9 +90,9 @@
 
 def link_kernel(
     rows, cols, sizes,
-    tile_rows, tile_cols, link_bonds, link_cells, tiles_live, links_live, bonds, ends_hbm, carry, stiffness,
-    table, ends_all, weight_all, cells_all,
-    ids, sem, row_send, row_recv,
+    tile_rows, tile_cols, link_bonds, link_cells, tiles_live, links_live, bonds, ends_hbm, carry, stiffness, tiles_hbm,
+    table, ends_all, weight_all, cells_all, tile_parts, tile_turned,
+    tiles, ids, sem, tile_sem, row_send, row_recv,
 ):
     link_slots, lanes = carry.shape
     width = ids.shape[1]
@@ -94,6 +102,8 @@
     barrier = greet(rows, cols, r, c, False)
     own_ends = pltpu.make_async_copy(ends_hbm, ends_all.at[r], sem.at[2])
     own_ends.start()
+    chunks = tile_sem.shape[0]
+    per_chunk = tiles.shape[0] // chunks
     ids[...] = jnp.zeros_like(ids)
     copies = []
     for i, (source, target) in enumerate((
@@ -105,8 +115,8 @@
     ids[2:3, 0:link_slots] = link_bonds[...]
     ids[3:4, 0:link_slots] = link_cells[...]
     tile_count, link_count = tiles_live[0], links_live[0]
-    slot = lax.broadcasted_iota(jnp.int32, (8, width), 1)
-    cells_all[r] = jnp.where(slot < link_count, jnp.broadcast_to(ids[3:4, :], (8, width)), -1)
+    slot = lax.broadcasted_iota(jnp.int32, (1, width), 1)
+    cells_all[r] = jnp.where(slot < link_count, ids[3:4, :], -1)
     for s in range(link_slots):
         live = jnp.full((1, lanes), s, jnp.int32) < link_count
         kept = jnp.where(live, carry[s : s + 1, :], 0).astype(jnp.float32)
@@ -116,6 +126,12 @@
     gathers = [
         row.gather_begin(phase, ends_hbm if phase == 0 else of(r), of) for phase, of in enumerate(slots)
     ]
+    tile_copies = []
+    for i in range(chunks):
+        part = pl.ds(i * per_chunk, per_chunk)
+        copy = pltpu.make_async_copy(tiles_hbm.at[part], tiles.at[part], tile_sem.at[i])
+        copy.start()
+        tile_copies.append(copy)
     for copy in copies:
         copy.wait()
     beyond = 1 << 20
@@ -146,9 +162,35 @@
         table[at + 4 : at + 5, :] = total(jnp.where(here, column(ids[other : other + 1, :]), 0), 0)
     table[20:22, :] = ids[2:4, :]
     table[22:24, :] = jnp.full((2, width), link_count, jnp.int32)
+
+    identity = jnp.where(
+        lax.broadcasted_iota(jnp.int32, (lanes, lanes), 0) == lax.broadcasted_iota(jnp.int32, (lanes, lanes), 1), 1.0, 0.0
+    ).astype(jnp.bfloat16)
+
+    def split_tiles(t, _):
+        high, low = halves(tiles[t])
+        tile_parts[t, 0:lanes, :] = high
+        tile_parts[t, lanes : 2 * lanes, :] = low
+        turned = dot(identity, jnp.concatenate([high, low], axis=0), NT)
+        tile_turned[t] = turned.astype(jnp.bfloat16)
+        return 0
+
+    def split_chunks(start, stop):
+        for i in range(start, stop):
+            tile_copies[i].wait()
+
+            def several(g, _):
+                for e in range(8):
+                    split_tiles(g * 8 + e, 0)
+                return 0
+
+            lax.fori_loop(i * per_chunk // 8, (i + 1) * per_chunk // 8, several, 0)
+
+    split_chunks(0, chunks // 2)
     own_ends.wait()
     for phase, of in enumerate(slots):
         row.gather_relay(phase, gathers[phase], of)
+    split_chunks(chunks // 2, chunks)
     for gather in gathers:
         row.gather_end(gather)
     for copy in started:
@@ -167,7 +209,7 @@
 
     def collect(i, found):
         for s in range(link_slots):
-            local = cells[i, s] - first
+            local = cells[i, 0, s] - first
             listed[found] = (i * link_slots + s) * cells_dev + local
             found = found + jnp.where((local >= 0) & (local < cells_dev), 1, 0)
         return found
@@ -216,14 +258,14 @@
 
 def kernel(
     rows, cols, sizes,
-    table, drive, hardness_hbm, stiffness_hbm, tiles_hbm, ends_hbm, carry_hbm, square, charge0, fixed, sums0,
+    table, drive, hardness_hbm, stiffness_hbm, tile_parts, tile_turned, ends_hbm, carry_hbm, square, charge0, fixed, sums0,
     out_solution, out_residual,
     hardness, stiffness, ends, carry,
-    tiles, tile_parts, incidence, u0, u1, u2, products, bond_products,
+    incidence, u0, u1, u2, products, bond_products,
     drive_all, row_charge, col_charge,
     row_parts, col_parts, pot_part, pot_in, mirror_part, mirror_in, pot_all, pot_parts,
     bond_part, bond_in, dots_row, dots_col,
-    small_sem, tile_sem, row_send, row_recv, col_send, col_recv,
+    small_sem, row_send, row_recv, col_send, col_recv,
 ):
     cells_dev, sets, lanes, tile_slots, link_slots, row_bonds = sizes
     group_cells, row_cells = rows * cells_dev, cols * cells_dev
@@ -242,33 +284,10 @@
         copy.start()
         small.append(copy)
     barrier = greet(rows, cols, r, c, True)
-    chunks = tile_sem.shape[0]
-    per_chunk = tile_slots // chunks
-    tile_copies = []
-    for i in range(chunks):
-        part = pl.ds(i * per_chunk, per_chunk)
-        copy = pltpu.make_async_copy(tiles_hbm.at[part], tiles.at[part], tile_sem.at[i])
-        copy.start()
-        tile_copies.append(copy)
     for l in range(cells_dev):
         part = slice(l * sets, (l + 1) * sets)
         col_charge[0, r, part, :] = charge0[l]
         row_charge[0, c, part, :] = charge0[l]
-    link_count = table[22, 0]
-    small[0].wait()
-    small[1].wait()
-
-    def build_incidence(s, _):
-        atom = lax.broadcasted_iota(jnp.int32, (lanes, lanes), 0)
-        pair = ends[s]
-        live = jnp.full((1, lanes), s, jnp.int32) < link_count
-        kept = jnp.where(live, carry[pl.ds(s, 1), :], 0).astype(jnp.float32)
-        gain = jnp.where(atom == pair[0:1, :], kept, 0.0)
-        lose = jnp.where(atom == pair[1:2, :], kept, 0.0)
-        incidence[s] = (gain - lose).astype(jnp.bfloat16)
-        return 0
-
-    lax.fori_loop(0, link_slots, build_incidence, 0)
     pl.semaphore_wait(barrier, rows + cols - 2)
 
     def send_row(phase, source, target):
@@ -295,12 +314,6 @@
         for copy in copies:
             copy.wait_recv()
 
-    def split_tiles(t, _):
-        high, low = halves(tiles[t])
-        tile_parts[t, 0:lanes, :] = high
-        tile_parts[t, lanes : 2 * lanes, :] = low
-        return 0
-
     UNROLL = 32
 
     def slot(s):
@@ -366,15 +379,15 @@
     def drive_slot(i):
         return drive_all.at[i]
 
-    def operate(n, background, prepare, middle, slack):
+    def operate(n, background, prepare, middle):
         def charge_slot(i):
             return col_charge.at[n, i]
 
         side = send_col(n, lambda peer: row_charge.at[n, c], row_charge.at[n, c])
         gather = row.gather_begin(3 * n, col_charge.at[n, r], charge_slot)
-        copies, other_slot, phase = background()
         prepare()
         arrive(side)
+        row.gather_relay(3 * n, gather, charge_slot, 1, 2)
         for k in range(cols):
             for l in range(cells_dev):
                 high, low = halves(row_charge[n, k, l * sets : (l + 1) * sets, :])
@@ -382,20 +395,19 @@
                 row_parts[k * cells_dev + l, sets : 2 * sets, :] = low
 
         def forward(k, t, cell):
-            both = dot(row_parts[cell], tile_parts[t], NT)
+            both = dot(row_parts[cell], tile_turned[t])
             return both[0:sets, 0:lanes] + (
                 both[sets : 2 * sets, 0:lanes] + both[0:sets, lanes : 2 * lanes]
             )
 
         half = tile_slots // (2 * UNROLL) * UNROLL
         carried = add_slots(0, forward, products, nothing, 0, half)
-        row.gather_relay(3 * n, gather, charge_slot)
+        row.gather_relay(3 * n, gather, charge_slot, 2)
+        copies, other_slot, phase = background()
         add_slots(0, forward, products, carried, half, tile_slots)
         spread_slots(0, group_cells, products, pot_part.at[n])
         parts = send_row(3 * n + 1, lambda peer: pot_part.at[n, row_block(peer)], pot_in.at[n, r])
         pot_in[n, r] = pot_part[n, row_block(r), :]
-        row.gather_relay(phase, copies, other_slot)
-        middle()
         row.gather_end(gather)
         for k in range(rows):
             for l in range(cells_dev):
@@ -414,8 +426,8 @@
         spread_slots(1, row_cells, products, mirror_part.at[n])
         side = send_col(2 + n, lambda peer: mirror_part.at[n, row_block(peer)], mirror_in.at[n, c])
         mirror_in[n, c] = mirror_part[n, row_block(c), :]
-        row.gather_end(copies)
-        slack()
+        middle()
+        row.gather_relay(phase, copies, other_slot)
         arrive(parts)
         total = pot_in[n, 0]
         for k in range(1, rows):
@@ -427,6 +439,7 @@
         for l in range(cells_dev):
             part = slice(l * sets, (l + 1) * sets)
             pot_all[n, r, part, :] = total[part] + hardness[l : l + 1, :] * own[part]
+        return copies
 
     def pot_slot(n):
         return lambda i: pot_all.at[n, i]
@@ -470,21 +483,34 @@
     def drive_background():
         return row.gather_begin(2, drive, drive_slot), drive_slot, 2
 
-    def prepare_tiles():
+    def finish_small():
+        link_count = table[22, 0]
+        small[0].wait()
+        small[1].wait()
+
+        def build_incidence(s, _):
+            atom = lax.broadcasted_iota(jnp.int32, (lanes, lanes), 0)
+            pair = ends[s]
+            live = jnp.full((1, lanes), s, jnp.int32) < link_count
+            kept = jnp.where(live, carry[pl.ds(s, 1), :], 0).astype(jnp.float32)
+            gain = jnp.where(atom == pair[0:1, :], kept, 0.0)
+            lose = jnp.where(atom == pair[1:2, :], kept, 0.0)
+            incidence[s] = (gain - lose).astype(jnp.bfloat16)
+            return 0
+
+        lax.fori_loop(0, link_slots, build_incidence, 0)
         for copy in small[2:]:
             copy.wait()
-        for i in range(chunks):
-            tile_copies[i].wait()
-            lax.fori_loop(i * per_chunk, (i + 1) * per_chunk, split_tiles, 0)
 
     def first_bonds():
+        row.gather_end(state["drive"])
         def first(s, value):
             u0[s] = -value
 
         to_bonds(lambda l: drive_all[l // cells_dev, lax.rem(l, cells_dev)], first)
         state["bonds0"] = send_bonds(0, u0)
 
-    operate(0, drive_background, prepare_tiles, lambda: None, first_bonds)
+    state["drive"] = operate(0, drive_background, finish_small, lambda: None)
 
     energy = sums0[1]
     for l in range(cells_dev):
@@ -507,7 +533,8 @@
     def first_dots():
         state["dots"] = dots_middle(0, state["dots"])
 
-    def second_bonds():
+    def second_bonds(copies):
+        row.gather_end(copies)
         def update(s, value):
             u1[s] = value + stiffness[pl.ds(table[20, s], 1), :] * u0[s]
 
@@ -528,8 +555,9 @@
 
         state["sums"] = lax.fori_loop(0, link_slots // 4, body, (nothing, nothing))
 
-    operate(1, potential_background, lambda: None, first_dots, second_bonds)
+    copies = operate(1, potential_background, first_bonds, first_dots)
     gather = row.gather_begin(6, pot_all.at[1, r], pot_slot(1))
+    second_bonds(copies)
     norm0, step0 = state["norm"], state["step"]
     norm_part, energy_part = state["sums"]
     for l in range(cells_dev):
@@ -595,28 +623,38 @@
     hbm = pl.BlockSpec(memory_space=pltpu.HBM)
     width = -(-max(tile_slots, link_slots, group_cells, row_bonds) // 128) * 128
     bonds = link_bonds.reshape(1, -1)
-    table, ends_all, weight_all, cells_all = pl.pallas_call(
+    coulomb_tiles, link_ends, link_carry, bond_stiffness, charge_drive, hardness, tile_rows, tile_cols, bonds, link_cells = (
+        pltpu.with_memory_space_constraint(x, pltpu.HBM) for x in
+        (coulomb_tiles, link_ends, link_carry, bond_stiffness, charge_drive, hardness,
+         tile_rows.reshape(1, -1), tile_cols.reshape(1, -1), bonds, link_cells.reshape(1, -1))
+    )
+    chunks = 8
+    table, ends_all, weight_all, cells_all, tile_parts, tile_turned = pl.pallas_call(
         functools.partial(link_kernel, rows, cols, None),
         out_shape=(
             jax.ShapeDtypeStruct((24, width), i32),
             jax.ShapeDtypeStruct((rows, *link_ends.shape), i32),
             jax.ShapeDtypeStruct((rows, link_slots, lanes), f32),
-            jax.ShapeDtypeStruct((rows, 8, width), i32),
+            jax.ShapeDtypeStruct((rows, 1, width), i32),
+            jax.ShapeDtypeStruct((tile_slots, 2 * lanes, lanes), bf16),
+            jax.ShapeDtypeStruct((tile_slots, lanes, 2 * lanes), bf16),
         ),
-        in_specs=[hbm] * 2 + [vmem] * 2 + [smem] * 3 + [hbm] + [vmem] * 2,
-        out_specs=(vmem,) * 4,
+        in_specs=[hbm] * 2 + [vmem] * 2 + [smem] * 3 + [hbm] + [vmem] * 2 + [hbm],
+        out_specs=(vmem,) * 6,
         scratch_shapes=[
+            pltpu.VMEM((tile_slots, lanes, lanes), f32),
             pltpu.VMEM((8, width), i32),
             pltpu.SemaphoreType.DMA((3,)),
+            pltpu.SemaphoreType.DMA((chunks,)),
             pltpu.SemaphoreType.DMA((3, rows)),
             pltpu.SemaphoreType.DMA((3, rows)),
         ],
         compiler_params=pltpu.CompilerParams(
-            collective_id=1, has_side_effects=True, vmem_limit_bytes=67043328
+            collective_id=1, has_side_effects=True, vmem_limit_bytes=32 << 20
         ),
     )(
-        tile_rows.reshape(1, -1), tile_cols.reshape(1, -1), bonds, link_cells.reshape(1, -1),
-        tile_count, link_count, bonds, link_ends, link_carry, bond_stiffness,
+        tile_rows, tile_cols, bonds, link_cells,
+        tile_count, link_count, bonds, link_ends, link_carry, bond_stiffness, coulomb_tiles,
     )
     square, charge0, fixed, sums0 = pl.pallas_call(
         functools.partial(cell_kernel, rows, (cells_dev, sets, lanes, link_slots)),
@@ -632,26 +670,23 @@
             pltpu.SMEM((rows * link_slots + 2 * GROUP,), i32),
             pltpu.VMEM((cells_dev, lanes + 4 * sets, lanes), f32),
         ],
-        compiler_params=pltpu.CompilerParams(vmem_limit_bytes=67043328),
+        compiler_params=pltpu.CompilerParams(vmem_limit_bytes=16 << 20),
     )(
-        cells_all[:, 0, :], ends_all.reshape(rows * link_slots, *link_ends.shape[1:]),
+        cells_all, ends_all.reshape(rows * link_slots, *link_ends.shape[1:]),
         weight_all.reshape(rows * link_slots, lanes), charge_drive,
     )
     out = jax.ShapeDtypeStruct((share, sets, lanes), f32)
     sizes = (cells_dev, sets, lanes, tile_slots, link_slots, row_bonds)
-    chunks = 8
     return pl.pallas_call(
         functools.partial(kernel, rows, cols, sizes),
         out_shape=(out, out),
-        in_specs=[smem] + [hbm] * 6 + [vmem] * 4,
+        in_specs=[smem] + [hbm] * 3 + [vmem] * 2 + [hbm] * 2 + [vmem] * 4,
         out_specs=(vmem, vmem),
         scratch_shapes=[
             pltpu.VMEM(hardness.shape, f32),
             pltpu.VMEM(bond_stiffness.shape, f32),
             pltpu.VMEM(link_ends.shape, i32),
             pltpu.VMEM(link_carry.shape, i32),
-            pltpu.VMEM((tile_slots, lanes, lanes), f32),
-            pltpu.VMEM((tile_slots, 2 * lanes, lanes), bf16),
             pltpu.VMEM((link_slots, lanes, lanes), bf16),
             pltpu.VMEM((link_slots, sets, lanes), f32),
             pltpu.VMEM((link_slots, sets, lanes), f32),
@@ -674,17 +709,16 @@
             pltpu.VMEM((2, rows, sets, lanes), f32),
             pltpu.VMEM((2, cols, sets, lanes), f32),
             pltpu.SemaphoreType.DMA((5,)),
-            pltpu.SemaphoreType.DMA((chunks,)),
             pltpu.SemaphoreType.DMA((9, rows)),
             pltpu.SemaphoreType.DMA((9, rows)),
             pltpu.SemaphoreType.DMA((9, cols)),
             pltpu.SemaphoreType.DMA((9, cols)),
         ],
         compiler_params=pltpu.CompilerParams(
-            collective_id=0, has_side_effects=True, vmem_limit_bytes=67043328
+            collective_id=0, has_side_effects=True, vmem_limit_bytes=32 << 20
         ),
     )(
-        table, charge_drive, hardness, bond_stiffness, coulomb_tiles, link_ends, link_carry,
+        table, charge_drive, hardness, bond_stiffness, tile_parts, tile_turned, link_ends, link_carry,
         square, charge0, fixed, sums0,
     )
 

time: 80.6 us -> 73.9 us (0.917)
  Pallas kernels: 74.4 us -> 70.4 us
  local copies, waits for them, and re-layouts: 4.31 us -> 1.26 us
    pallas_call x1, Pallas kernels: 55.4 us -> 50.6 us  [on_device(): pl.pallas_call(functools.partial(kernel, rows, cols, sizes), out_shape=(o...]
    unnamed x2, local copies, waits for them, and re-layouts: 2.95 us -> 1.26 us
    pallas_call x1, Pallas kernels: 4.29 us -> 5.44 us  [on_device(): pl.pallas_call(functools.partial(cell_kernel, rows, (cells_dev, sets, lan...]
where the time goes in v2:
time: 73.9 us; the launch traced here: 73.6 us
  Pallas kernels  70.4 us (95%)
  between operations  1.95 us (3%)
  local copies, waits for them, and re-layouts  1.26 us (2%)
    pallas_call x1, Pallas kernels, on_device(): pl.pallas_call(functools.partial(kernel, rows, cols, sizes), out_shape=(o...  50.6 us
    pallas_call x1, Pallas kernels, on_device(): pl.pallas_call(functools.partial(link_kernel, rows, cols, None), out_shap...  14.3 us
    pallas_call x1, Pallas kernels, on_device(): pl.pallas_call(functools.partial(cell_kernel, rows, (cells_dev, sets, lan...  5.44 us

profile of v2, /device:TPU:1, one launch (start us, length us, event | category | flops | bytes accessed | tf_op | source)
XLA Modules:
  0.0 73.6 jit_solution(6232611398623665802)
XLA Ops:
  1.9 14.3 %shard_map.131 = (s32[24,128]{1,0:T(8,128)S(1)}, s32[8,32,2,128]{3,2,1,0:T(2,128)S(1)}, f32[8,32,128]{2,1,0:T(8,128)S(1)}, s32[8,1,128]{2,1,0:T(1,128)S(1)}, bf1...) custom-call(s32[1,128]{1,0:T(1,128)} %bitcast.10, s32[1,128]{1,0:T(1,128)} %bitcast.11, ...), custom_call_target="tpu_custom_call" | custom-call | tf_op jit(solution)/shard_map/pallas_call | solution.py:632
  16.2 5.4 %shard_map.132 = (bf16[4,128,256]{2,1,0:T(8,128)(2,1)S(1)}, f32[4,16,128]{2,1,0:T(8,128)S(1)}, f32[4,16,128]{2,1,0:T(8,128)S(1)}, f32[2,16,128]{2,1,0:T(8,128)S(1)}) custom-call(s32[8,1,128]{2,1,0:T(1,128)S(1)} %get-tuple-element.15.cells, s32[256,2,128]{2,1,0:T(2,128)S(1)} %bitcast.6, f32[256,128]{1,0:T(8,128)S(1)} %bitcast.7, f32[4,16,128]{2,1,0:T(8,128)} %drive.3), custom_call_target="tpu_custom_call" | custom-call | tf_op jit(solution)/shard_map/pallas_call | solution.py:659
  21.7 50.6 %shard_map.133 = (f32[8,16,128]{2,1,0:T(8,128)S(1)}, f32[8,16,128]{2,1,0:T(8,128)S(1)}) custom-call(s32[24,128]{1,0:T(8,128)S(1)} %get-tuple-element.12.table, f32[4,16,128]{2,1,0:T(8,128)} %drive.3, f32[4,128]{1,0:T(4,128)} %hardness_hbm.1, f32[32,128]{1,0:T(8,128)} %stiffness_hbm.1, bf16[128,256,128]{2,1,0:T(8,128)(2,1)S(1)} %get-tuple-element.13.tile_parts, ...), custom_call_target="tpu_custom_call" | custom-call | tf_op jit(solution)/shard_map/pallas_call | solution.py:680
  72.3 0.6 copy.18
  72.9 0.6 copy.19

commit v3 on v2

--- a/solution.py
+++ b/solution.py
@@ -186,18 +186,18 @@
 
             lax.fori_loop(i * per_chunk // 8, (i + 1) * per_chunk // 8, several, 0)
 
-    split_chunks(0, chunks // 2)
+    split_chunks(0, chunks * 5 // 8)
     own_ends.wait()
     for phase, of in enumerate(slots):
         row.gather_relay(phase, gathers[phase], of)
-    split_chunks(chunks // 2, chunks)
+    split_chunks(chunks * 5 // 8, chunks)
     for gather in gathers:
         row.gather_end(gather)
     for copy in started:
         copy.wait_send()
 
 
-GROUP = 4
+GROUP = 8
 
 
 def cell_kernel(
@@ -291,10 +291,11 @@
     pl.semaphore_wait(barrier, rows + cols - 2)
 
     def send_row(phase, source, target):
-        return [
-            row.copy(phase, k, source(lax.rem(r + k, rows)), target, lax.rem(r + k, rows))
-            for k in range(1, rows)
-        ]
+        copies = []
+        for k in range(rows - 1, 0, -1):
+            peer = row.partner(k // row.inner) * row.inner + lax.rem(row.low + k % row.inner, row.inner)
+            copies.append(row.copy(phase, k, source(peer), target, peer))
+        return copies
 
     def send_col(phase, source, target):
         copies = []
@@ -385,6 +386,7 @@
 
         side = send_col(n, lambda peer: row_charge.at[n, c], row_charge.at[n, c])
         gather = row.gather_begin(3 * n, col_charge.at[n, r], charge_slot)
+        copies, other_slot, phase = background()
         prepare()
         arrive(side)
         row.gather_relay(3 * n, gather, charge_slot, 1, 2)
@@ -403,7 +405,6 @@
         half = tile_slots // (2 * UNROLL) * UNROLL
         carried = add_slots(0, forward, products, nothing, 0, half)
         row.gather_relay(3 * n, gather, charge_slot, 2)
-        copies, other_slot, phase = background()
         add_slots(0, forward, products, carried, half, tile_slots)
         spread_slots(0, group_cells, products, pot_part.at[n])
         parts = send_row(3 * n + 1, lambda peer: pot_part.at[n, row_block(peer)], pot_in.at[n, r])
@@ -426,8 +427,8 @@
         spread_slots(1, row_cells, products, mirror_part.at[n])
         side = send_col(2 + n, lambda peer: mirror_part.at[n, row_block(peer)], mirror_in.at[n, c])
         mirror_in[n, c] = mirror_part[n, row_block(c), :]
+        row.gather_relay(phase, copies, other_slot)
         middle()
-        row.gather_relay(phase, copies, other_slot)
         arrive(parts)
         total = pot_in[n, 0]
         for k in range(1, rows):

time: 73.9 us -> 70.6 us (0.955)
  Pallas kernels: 70.4 us -> 66.8 us
    pallas_call x1, Pallas kernels: 50.6 us -> 48.3 us  [on_device(): pl.pallas_call(functools.partial(kernel, rows, cols, sizes), out_shape=(o...]
    pallas_call x1, Pallas kernels: 5.44 us -> 4.12 us  [on_device(): pl.pallas_call(functools.partial(cell_kernel, rows, (cells_dev, sets, lan...]
where the time goes in v3:
time: 70.6 us; the launch traced here: 70 us
  Pallas kernels  66.8 us (95%)
  between operations  1.95 us (3%)
  local copies, waits for them, and re-layouts  1.26 us (2%)
    pallas_call x1, Pallas kernels, on_device(): pl.pallas_call(functools.partial(kernel, rows, cols, sizes), out_shape=(o...  48.3 us
    pallas_call x1, Pallas kernels, on_device(): pl.pallas_call(functools.partial(link_kernel, rows, cols, None), out_shap...  14.4 us
    pallas_call x1, Pallas kernels, on_device(): pl.pallas_call(functools.partial(cell_kernel, rows, (cells_dev, sets, lan...  4.12 us

profile of v3, /device:TPU:1, one launch (start us, length us, event | category | flops | bytes accessed | tf_op | source)
XLA Modules:
  0.0 70.0 jit_solution(17140363572077654581)
XLA Ops:
  1.9 14.4 %shard_map.131 = (s32[24,128]{1,0:T(8,128)S(1)}, s32[8,32,2,128]{3,2,1,0:T(2,128)S(1)}, f32[8,32,128]{2,1,0:T(8,128)S(1)}, s32[8,1,128]{2,1,0:T(1,128)S(1)}, bf1...) custom-call(s32[1,128]{1,0:T(1,128)} %bitcast.10, s32[1,128]{1,0:T(1,128)} %bitcast.11, ...), custom_call_target="tpu_custom_call" | custom-call | tf_op jit(solution)/shard_map/pallas_call | solution.py:633
  16.3 4.1 %shard_map.132 = (bf16[4,128,256]{2,1,0:T(8,128)(2,1)S(1)}, f32[4,16,128]{2,1,0:T(8,128)S(1)}, f32[4,16,128]{2,1,0:T(8,128)S(1)}, f32[2,16,128]{2,1,0:T(8,128)S(1)}) custom-call(s32[8,1,128]{2,1,0:T(1,128)S(1)} %get-tuple-element.15.cells, s32[256,2,128]{2,1,0:T(2,128)S(1)} %bitcast.6, f32[256,128]{1,0:T(8,128)S(1)} %bitcast.7, f32[4,16,128]{2,1,0:T(8,128)} %drive.3), custom_call_target="tpu_custom_call" | custom-call | tf_op jit(solution)/shard_map/pallas_call | solution.py:660
  20.4 48.3 %shard_map.133 = (f32[8,16,128]{2,1,0:T(8,128)S(1)}, f32[8,16,128]{2,1,0:T(8,128)S(1)}) custom-call(s32[24,128]{1,0:T(8,128)S(1)} %get-tuple-element.12.table, f32[4,16,128]{2,1,0:T(8,128)} %drive.3, f32[4,128]{1,0:T(4,128)} %hardness_hbm.1, f32[32,128]{1,0:T(8,128)} %stiffness_hbm.1, bf16[128,256,128]{2,1,0:T(8,128)(2,1)S(1)} %get-tuple-element.13.tile_parts, ...), custom_call_target="tpu_custom_call" | custom-call | tf_op jit(solution)/shard_map/pallas_call | solution.py:681
  68.7 0.6 copy.18
  69.4 0.6 copy.19
